TPU v7x, 512 devices: a whole 4x4x16 slice. The times are simulated.
512 devices in a mesh: strata: 32 (over z, x_lo), shard: 16 (over y, x_hi, core).
Axes of the slice: x: 4 (x_hi: 2, x_lo: 2; x = x_hi * 2 + x_lo), y: 4, z: 16, core: 2. Of those that a mesh axis runs over, the one named last changes fastest.
Arguments:
- user_factors: bfloat16 [524288, 512], P(('strata', 'shard')), may hold values from -1.1953125 to 1.1953125
- item_factors: float32 [16384, 512], P(('strata', 'shard')), may hold values from -1.2 to 1.2
- tile_blocks: int32 [32, 16, 3, 8, 2], P('strata', 'shard'), may hold values from 0 to 7, as said below
- tile_counts: int32 [32, 16, 3], P('strata', 'shard'), may hold values from 1 to 8, as said below
- ratings: bfloat16 [32, 16, 3, 8, 128, 128], P('strata', 'shard'), may hold values from -5 to 5
- mask_words: int32 [32, 16, 3, 8, 16, 128], P('strata', 'shard'), may hold values from 0 to 255
Outputs:
- users_out: bfloat16 [524288, 512], P(('strata', 'shard'))
- items_out: float32 [16384, 512], P(('strata', 'shard'))
Inputs may be any that keep to these rules, and one draw needn't show every extreme that they name: `tile_blocks`: entry 0 is a user block below 8, entry 1 an item block below 4; the 8 pairs of one stratum, shard and visit are distinct. `tile_counts`: some stratum, shard and visit has exactly 8 live slots in every draw.
All inputs are finite; a program needn't handle non-finite values.
Results may differ from a plain program's by a relative error of at most 0.0095.
Values may be sent and summed in bfloat16 or wider, within the bound.
A program may use at most 64 MiB of HBM per device.

v0:
```python
import jax
import jax.numpy as jnp
from jax import lax
from jax.sharding import PartitionSpec as P

step_user = 0.05
step_item = 0.004
shrinkage = 0.05


def shifted(x, axis, by):
    peers = lax.axis_size(axis)
    return lax.ppermute(x, axis, [(i, (i + by) % peers) for i in range(peers)])


def unpack_mask(words):
    shifts = jnp.arange(8, dtype=jnp.int32)
    bits = jnp.bitwise_and(jnp.right_shift(words[:, :, None, :], shifts[None, None, :, None]), 1)
    return bits.reshape(words.shape[0], words.shape[1] * 8, words.shape[2]).astype(jnp.float32)


def device_terms(users, panel_low, blocks, count, rates, words):
    tile_side = rates.shape[-1]
    width = users.shape[1]
    user_count = users.shape[0] // tile_side
    item_count = panel_low.shape[0] // tile_side
    live = (jnp.arange(blocks.shape[0], dtype=jnp.int32) < count).astype(jnp.float32)
    weights = unpack_mask(words) * live[:, None, None]
    user_rows = jnp.take(users.reshape(user_count, tile_side, width), blocks[:, 0], axis=0)
    item_rows = jnp.take(panel_low.reshape(item_count, tile_side, width), blocks[:, 1], axis=0)
    predicted = jnp.einsum("kur,kir->kui", user_rows, item_rows, preferred_element_type=jnp.float32)
    error_tile = (weights * (rates.astype(jnp.float32) - predicted)).astype(jnp.bfloat16)
    user_terms = jnp.einsum(
        "kui,kir->kur", error_tile, item_rows, preferred_element_type=jnp.float32
    )
    item_terms = jnp.einsum(
        "kui,kur->kir", error_tile, user_rows, preferred_element_type=jnp.float32
    )
    user_hot = (blocks[:, 0][:, None] == jnp.arange(user_count, dtype=jnp.int32)[None, :]).astype(
        jnp.float32
    )
    item_hot = (blocks[:, 1][:, None] == jnp.arange(item_count, dtype=jnp.int32)[None, :]).astype(
        jnp.float32
    )
    grad_user = jnp.einsum(
        "kb,kur->bur", user_hot, user_terms, precision=lax.Precision.HIGHEST
    ).reshape(-1, width)
    grad_item = jnp.einsum(
        "kb,kir->bir", item_hot, item_terms, precision=lax.Precision.HIGHEST
    ).reshape(-1, width)
    return (grad_user, grad_item)


def shards(user_factors, item_factors, tile_blocks, tile_counts, ratings, mask_words):
    blocks_all = tile_blocks[0, 0]
    counts_all = tile_counts[0, 0]
    rates_all = ratings[0, 0]
    words_all = mask_words[0, 0]
    visits = counts_all.shape[0]
    users = user_factors
    panel = item_factors
    for visit in range(visits):
        panel_low = lax.all_gather(panel.astype(jnp.bfloat16), "shard", axis=0, tiled=True)
        grad_user, grad_item = device_terms(
            users,
            panel_low,
            blocks_all[visit],
            counts_all[visit],
            rates_all[visit],
            words_all[visit],
        )
        summed = lax.psum_scatter(
            grad_item.astype(jnp.bfloat16), "shard", scatter_dimension=0, tiled=True
        ).astype(jnp.float32)
        factor = users.astype(jnp.float32)
        users = (factor + step_user * (grad_user - shrinkage * factor)).astype(jnp.bfloat16)
        panel = panel + step_item * (summed - shrinkage * panel)
        if visit + 1 < visits:
            panel = shifted(panel.astype(jnp.bfloat16), "strata", 1).astype(panel.dtype)
    return (users, panel)


def solution(mesh):
    placed = (
        P(("strata", "shard"), None),
        P(("strata", "shard"), None),
        P("strata", "shard", None, None, None),
        P("strata", "shard", None),
        P("strata", "shard", None, None, None, None),
        P("strata", "shard", None, None, None, None),
    )
    return jax.shard_map(
        shards,
        mesh=mesh,
        in_specs=placed,
        out_specs=(P(("strata", "shard"), None), P(("strata", "shard"), None)),
        check_vma=False,
    )
```

profile of v0, /device:TPU:1, one launch (start us, length us, event | category | flops | bytes accessed | tf_op | source)
XLA Modules:
  0.0 392.9 jit_solution(7805216325913225970)
XLA Ops:
  7.2 0.0 reduce-scatter.4.cloned.1.call-start
  7.2 0.8 slice_bitcast_fusion.3
  8.0 0.5 slice_bitcast_fusion.10
  8.5 0.6 compare_and_fusion.4
  9.1 1.4 fusion.83
  10.6 1.2 compare_convert_fusion.2
  11.8 0.6 shift_right_arithmetic.70
  12.4 0.8 convert_element_type.130
  13.2 1.5 slice_bitcast_fusion
  14.7 28.6 %all_gather.9 = bf16[512,512]{1,0:T(8,128)(2,1)S(1)} all-gather(bf16[32,512]{1,0:T(8,128)(2,1)S(1)} %convert_element_type.130), channel_id=1, replica_groups=mesh['strata'=32,'shard'=16] {'shard'}, dimensions={0}, use_global_device_ids=true | all-gather | bytes 557056 | tf_op jit(solution)/shard_map/all_gather | solution.py:63
  43.4 0.6 gather_fusion.1
  44.0 0.6 gather_fusion
  44.6 0.0 copy-start.5
  44.6 1.5 fusion.35
  46.2 0.5 fusion.45
  46.7 0.1 copy-done.6
  46.8 2.2 fusion.21
  49.0 0.9 copy.9
  49.9 0.0 reduce-scatter.4.cloned.1.call-update
  49.9 0.0 reduce-scatter.6.cloned.1.call-start
  50.0 0.5 fusion.46
  50.5 2.2 fusion.19
  52.8 1.2 copy.8
  54.0 0.0 copy-start.3
  54.0 0.4 fusion.2
  54.5 80.8 %reduce-scatter.4.cloned.1.call-done = bf16[32,512]{1,0:T(8,128)(2,1)} async-done(((bf16[512,512]{1,0:T(8,128)(2,1)}), bf16[32,512]{1,0:T(8,128)(2,1)}) %reduce-scatter.4.cloned.1.call-update) | async-done | bytes 32784 | tf_op jit(solution)/shard_map/reduce_scatter | solution.py:72
  135.2 0.8 add_convert_fusion
  136.0 2.7 collective-permute-start
  138.7 0.6 compare_convert_fusion.1
  139.3 1.6 gather_fusion.2
  140.9 2.5 collective-permute-done
  143.4 28.1 %all_gather.10 = bf16[512,512]{1,0:T(8,128)(2,1)S(1)} all-gather(bf16[32,512]{1,0:T(8,128)(2,1)S(1)} %collective-permute-done), channel_id=1, replica_groups=mesh['strata'=32,'shard'=16] {'shard'}, dimensions={0}, use_global_device_ids=true | all-gather | bytes 557056 | tf_op jit(solution)/shard_map/all_gather | solution.py:63
  171.6 0.6 gather_fusion.3
  172.2 0.0 copy-start.1
  172.2 1.9 fusion.34
  174.1 0.5 fusion.47
  174.6 2.2 fusion.24
  176.8 0.9 copy.11
  177.7 0.0 reduce-scatter.6.cloned.1.call-update
  177.8 0.0 reduce-scatter.8.cloned.1.call-start
  177.8 0.6 compare_convert_fusion
  178.5 0.5 fusion.48
  179.0 2.2 fusion.15
  181.2 2.5 copy.10
  183.7 76.3 %reduce-scatter.6.cloned.1.call-done = bf16[32,512]{1,0:T(8,128)(2,1)} async-done(((bf16[512,512]{1,0:T(8,128)(2,1)}), bf16[32,512]{1,0:T(8,128)(2,1)}) %reduce-scatter.6.cloned.1.call-update) | async-done | bytes 32784 | tf_op jit(solution)/shard_map/reduce_scatter | solution.py:72
  260.1 0.8 fusion.53
  260.8 2.6 collective-permute-start.1
  263.5 2.0 fusion.5
  265.5 1.6 gather_fusion.4
  267.1 1.2 collective-permute-done.1
  268.3 28.2 %all_gather.11 = bf16[512,512]{1,0:T(8,128)(2,1)S(1)} all-gather(bf16[32,512]{1,0:T(8,128)(2,1)S(1)} %collective-permute-done.1), channel_id=1, replica_groups=mesh['strata'=32,'shard'=16] {'shard'}, dimensions={0}, use_global_device_ids=true | all-gather | bytes 557056 | tf_op jit(solution)/shard_map/all_gather | solution.py:63
  296.4 0.6 gather_fusion.5
  297.0 0.0 copy-start
  297.1 1.9 fusion.33
  299.0 0.5 fusion.49
  299.5 2.2 fusion.27
  301.7 0.9 copy.13
  302.6 0.0 reduce-scatter.8.cloned.1.call-update
  302.6 0.5 fusion.50
  303.1 2.2 fusion.11
  305.4 1.2 copy.12
  306.6 1.4 fusion.8
  308.0 76.9 %reduce-scatter.8.cloned.1.call-done = bf16[32,512]{1,0:T(8,128)(2,1)} async-done(((bf16[512,512]{1,0:T(8,128)(2,1)}), bf16[32,512]{1,0:T(8,128)(2,1)}) %reduce-scatter.8.cloned.1.call-update) | async-done | bytes 32784 | tf_op jit(solution)/shard_map/reduce_scatter | solution.py:72
  385.0 1.4 convert_add_fusion.3
  (18 shorter events, 0.1 us)
Async XLA Ops:
  7.2 36.8 %copy-start.2 = (bf16[1024,512]{1,0:T(8,128)(2,1)S(1)}, bf16[1024,512]{1,0:T(8,128)(2,1)}, u32[]{:S(2)}) copy-start(bf16[1024,512]{1,0:T(8,128)(2,1)} %param.10) | copy-start | bytes 3145732
  7.2 128.1 %reduce-scatter.4.cloned.1.call-start = ((), (), s32[]{:S(2)}) async-start(), calls=%async_computation.3 | async-start | bytes 557056 | tf_op jit(solution)/shard_map/reduce_scatter | solution.py:72
  44.6 1.5 copy-start.5
  46.2 0.6 copy-start.6
  46.8 3.2 copy-start.4
  49.9 210.1 %reduce-scatter.6.cloned.1.call-start = ((), (), s32[]{:S(2)}) async-start(), calls=%async_computation.4 | async-start | bytes 557056 | tf_op jit(solution)/shard_map/reduce_scatter | solution.py:72
  54.0 81.2 %copy-start.3 = (f32[32,512]{1,0:T(8,128)S(1)}, f32[32,512]{1,0:T(8,128)}, u32[]{:S(2)}) copy-start(f32[32,512]{1,0:T(8,128)} %param.11) | copy-start | bytes 196612
  136.0 7.4 %collective-permute-start = (bf16[32,512]{1,0:T(8,128)(2,1)S(1)}, bf16[32,512]{1,0:T(8,128)(2,1)S(1)}, u32[]{:S(2)}, u32[]{:S(2)}) collective-permute-start(bf16[32,512]{1,0:T(8,128)(2,1)S(1)} %add_convert_fusion), channel_id=1, source_target_pairs={{0,16},{16,32},{32,48},{48,64},{64,80},{80,96},{96,112},{112,128},... | collective-permute-start | bytes 98312 | tf_op jit(solution)/shard_map/ppermute | solution.py:13
  139.3 32.9 %copy-start.7 = (s32[128]{0:T(128)S(1)}, s32[128]{0:T(128)}, u32[]{:S(2)}) copy-start(s32[128]{0:T(128)} %shift_right_arithmetic.70) | copy-start | bytes 1540
  172.2 1.9 copy-start.1
  177.8 207.2 %reduce-scatter.8.cloned.1.call-start = ((), (), s32[]{:S(2)}) async-start(), calls=%async_computation.5 | async-start | bytes 557056 | tf_op jit(solution)/shard_map/reduce_scatter | solution.py:72
  260.8 7.4 %collective-permute-start.1 = (bf16[32,512]{1,0:T(8,128)(2,1)S(1)}, bf16[32,512]{1,0:T(8,128)(2,1)S(1)}, u32[]{:S(2)}, u32[]{:S(2)}) collective-permute-start(bf16[32,512]{1,0:T(8,128)(2,1)S(1)} %fusion.53), channel_id=1, source_target_pairs={{0,16},{16,32},{32,48},{48,64},{64,80},{80,96},{96,112},{112,128},... | collective-permute-start | bytes 98312 | tf_op jit(solution)/shard_map/ppermute | solution.py:13
  297.0 1.9 copy-start
Sparse Core Ops, SparseCore 0:
  50.0 85.1 reduce-scatter.3
  177.9 82.1 reduce-scatter.5
  302.8 82.1 reduce-scatter.7
where the time goes:
time: 394 us; the launch traced here: 393 us
  waiting for transfers between devices  238 us (60%)
  blocking collectives  84.9 us (22%)
  matrix products  21.6 us (5%)
  local copies, waits for them, and re-layouts  18.3 us (5%)
  between operations  14.1 us (4%)
  other arithmetic  10.7 us (3%)
  starting transfers between devices  5.43 us (1%)
    reduce_scatter x3, waiting for transfers between devices, shards(): lax.psum_scatter(grad_item.astype(jnp.bfloat16), 'shard', scatter_dimensi...  234 us
    all_gather x3, blocking collectives, shards(): lax.all_gather(panel.astype(jnp.bfloat16), 'shard', axis=0, tiled=True)  84.9 us
  transfers between devices with their start and end apart: 5, of which 5 were waited for; matrix products, arithmetic and copies ran while one was open for 5% of the time, Pallas kernels for 0%

commit v1 on v0

v1 whole, which is shorter than its diff:
```python
import jax
import jax.numpy as jnp
from jax import lax
from jax.experimental import pallas as pl
from jax.experimental.pallas import tpu as pltpu
from jax.sharding import PartitionSpec as P

MESH = pl.DeviceIdType.MESH
BF = jnp.bfloat16
F32 = jnp.float32

step_user = 0.05
step_item = 0.004
shrinkage = 0.05

NY, NX, NC = 4, 2, 2
T, K, SIDE, R = 3, 8, 128, 512
J, W = 2, 256
PIECE = 32
UB, IB = 8, 4
N_STRATA = 32


def kernel(
    blocks, counts, users_in, items, ratings_in, words_in,
    users_out, items_out,
    users, ratings, words, panel, err, err_t, dense, dense_t, grads,
    c_out, c_in, y_out, y_in, x_out, x_in, f_out, f_in,
    load_sem, c_send, c_recv, y_send, y_recv, x_send, x_recv, f_send, f_recv,
    g_send, g_recv, p_send, p_recv, i_send, i_recv,
):
    s = lax.axis_index("strata")
    h = lax.axis_index("shard")
    y = h // 4
    x = (h // 2) % 2
    c = h % 2
    after = lax.rem(s + 1, N_STRATA)
    before = lax.rem(s + N_STRATA - 1, N_STRATA)

    def shard_of(yy, xx, cc):
        return yy * 4 + xx * 2 + cc

    def row(dy):
        return lax.rem(y + dy, NY)

    mate = (s, shard_of(y, x, 1 - c))

    loads = [
        pltpu.make_async_copy(users_in, users, load_sem.at[0]),
        pltpu.make_async_copy(ratings_in, ratings, load_sem.at[1]),
        pltpu.make_async_copy(words_in, words, load_sem.at[2]),
    ]
    for load in loads:
        load.start()

    barrier = pltpu.get_barrier_semaphore()
    partners = [mate, (s, shard_of(y, 1 - x, c))]
    partners += [(s, shard_of(row(dy), x, c)) for dy in (1, 2, 3)]
    partners += [(after, shard_of(y, xx, c)) for xx in range(NX)]
    partners += [(before, shard_of(y, xx, c)) for xx in range(NX)]
    for partner in partners:
        pl.semaphore_signal(barrier, inc=1, device_id=partner, device_id_type=MESH)

    for j in range(J):
        panel[0, j, y, x, c] = items[:, j * W:(j + 1) * W].astype(BF)

    pl.semaphore_wait(barrier, len(partners))

    def remote(src, dst, send, recv, to):
        return pltpu.make_async_remote_copy(
            src_ref=src, dst_ref=dst, send_sem=send, recv_sem=recv, device_id=to, device_id_type=MESH
        )

    def first_copy(j, xx):
        part = panel.at[0, j, y, xx, c]
        return remote(part, part, i_send.at[j], i_recv.at[j], (s, shard_of(y, 1 - x, c)))

    def gather_y(t, j, dy, yy):
        part = panel.at[t, j, yy, :, c]
        return remote(part, part, g_send.at[t, j, dy - 1], g_recv.at[t, j, dy - 1], (s, shard_of(row(dy), x, c)))

    def gather_c(t, j, dy, cc):
        part = panel.at[t, j, row(4 - dy), :, cc]
        return remote(part, part, p_send.at[t, j, dy], p_recv.at[t, j, dy], mate)

    def reduce_c(t, j):
        return remote(c_out.at[t, j], c_in.at[t, j], c_send.at[t, j], c_recv.at[t, j], mate)

    def reduce_y(t, j, dy):
        return remote(
            y_out.at[t, j, dy - 1], y_in.at[t, j, dy - 1], y_send.at[t, j, dy - 1], y_recv.at[t, j, dy - 1],
            (s, shard_of(row(dy), x, c)),
        )

    def advance(t, j, xx, slot):
        return remote(
            x_out.at[t, j], x_in.at[t, j, slot], x_send.at[t, j, xx], x_recv.at[t, j, slot],
            (after, shard_of(y, xx, c)),
        )

    def last_copy(j):
        return remote(f_out.at[j], f_in.at[j], f_send.at[j], f_recv.at[j], (s, shard_of(y, 1 - x, c)))

    def gather_start(t, j):
        for dy in (2, 1, 3):
            gather_y(t, j, dy, y).start()
        gather_c(t, j, 0, c).start()

    def gather_finish(t):
        for j in range(J):
            for dy in (1, 3, 2):
                gather_y(t, j, dy, row(4 - dy)).wait_recv()
                gather_c(t, j, dy, c).start()
        for j in range(J):
            for dy in range(NY):
                gather_c(t, j, dy, 1 - c).wait_recv()

    for j in range(J):
        first_copy(j, x).start()

    def slots_of(t):
        cells = [blocks[t * 2 * K + 2 * k] * IB + blocks[t * 2 * K + 2 * k + 1] for k in range(K)]
        found = []
        for cell in range(UB * IB):
            rank = (cells[0] == cell).astype(jnp.int32) * K
            for k in range(1, K):
                rank = jnp.maximum(rank, (cells[k] == cell).astype(jnp.int32) * (K - k))
            found.append(K - rank)
        return found

    err[K] = jnp.zeros((SIDE, SIDE), BF)
    err_t[K] = jnp.zeros((SIDE, SIDE), BF)

    for j in range(J):
        first_copy(j, 1 - x).wait_recv()
        gather_start(0, j)
    for load in loads:
        load.wait()
    gather_finish(0)

    bit = lax.broadcasted_iota(jnp.int32, (16, 8, SIDE), 1)

    def tile_error(t, k):
        at = blocks[t * 2 * K + 2 * k]
        item = blocks[t * 2 * K + 2 * k + 1]
        live = (k < counts[t]).astype(jnp.int32)
        predicted = jnp.zeros((SIDE, SIDE), F32)
        for j in range(J):
            rows = panel[t, j, item].reshape(SIDE, W)
            predicted += lax.dot_general(
                users[at, :, j * W:(j + 1) * W], rows, (((1,), (1,)), ((), ())), preferred_element_type=F32
            )
        mask = jnp.bitwise_and(jnp.right_shift(words[t * K + k][:, None, :], bit), live).reshape(SIDE, SIDE)
        error = jnp.where(mask != 0, ratings[t * K + k].astype(F32) - predicted, 0.0)
        err[k] = error.astype(BF)
        err_t[k] = error.T.astype(BF)

    def reduce_pair(t, j):
        for dy in (2, 1, 3):
            yy = row(dy)
            y_out[t, j, dy - 1] = (grads[j, yy, :, c] + c_in[t, j, yy].astype(F32)).astype(BF)
            reduce_y(t, j, dy).start()

    def reduced(t, j):
        total = grads[j, y, :, c] + c_in[t, j, y].astype(F32)
        for dy in (1, 3, 2):
            reduce_y(t, j, dy).wait_recv()
            total += y_in[t, j, dy - 1].astype(F32)
        return total

    def update_users(t, j):
        columns = slice(j * W, (j + 1) * W)
        grad = jnp.dot(dense[...], panel[t, j].reshape(IB * SIDE, W), preferred_element_type=F32)
        grad = grad.reshape(UB, SIDE, W)
        factor = users[:, :, columns].astype(F32)
        users[:, :, columns] = (factor + step_user * (grad - shrinkage * factor)).astype(BF)

    def visit(t, last):
        for k in range(K):
            tile_error(t, k)
        slots = slots_of(t)
        for b in range(IB):
            for a in range(UB):
                slot = slots[a * IB + b]
                dense_t[b * SIDE:(b + 1) * SIDE, a * SIDE:(a + 1) * SIDE] = err_t[slot]
        for j in range(J):
            grads[j] = jnp.dot(
                dense_t[...], users[:, :, j * W:(j + 1) * W].reshape(UB * SIDE, W), preferred_element_type=F32
            ).reshape(NY, NX, NC, PIECE, W)
            c_out[t, j] = grads[j, :, :, 1 - c].astype(BF)
            reduce_c(t, j).start()
        for b in range(IB):
            for a in range(UB):
                slot = slots[a * IB + b]
                dense[a * SIDE:(a + 1) * SIDE, b * SIDE:(b + 1) * SIDE] = err[slot]
        for j in range(J):
            reduce_c(t, j).wait_recv()
            reduce_pair(t, j)
        update_users(t, 0)
        if not last:
            for j in range(J):
                total = reduced(t, j)
                mine = panel[t, j, y, :, c].astype(F32)
                half = step_item * total + (0.5 * (1.0 - step_item * shrinkage)) * mine
                x_out[t, j] = half.astype(BF)
                for xx in range(NX):
                    advance(t, j, xx, x).start()
            update_users(t, 1)
            for j in range(J):
                for xx in range(NX):
                    advance(t, j, xx, xx).wait_recv()
                both = x_in[t, j, 0].astype(F32) + x_in[t, j, 1].astype(F32)
                panel[t + 1, j, y, :, c] = both.astype(BF)
                gather_start(t + 1, j)
            gather_finish(t + 1)
        else:
            for j in range(J):
                grads[j, y, :, c] = reduced(t, j)
                f_out[j] = grads[j, y, 1 - x, c].astype(BF)
                last_copy(j).start()
            update_users(t, 1)
            out = pltpu.make_async_copy(users, users_out, load_sem.at[0])
            out.start()
            for j in range(J):
                last_copy(j).wait_recv()
                total = grads[j, y, x, c] + f_in[j].astype(F32)
                mine = panel[t, j, y, x, c].astype(F32)
                items_out[:, j * W:(j + 1) * W] = mine + step_item * (total - shrinkage * mine)
            out.wait()

    for t in range(T):
        visit(t, t == T - 1)

    for j in range(J):
        first_copy(j, x).wait_send()
        last_copy(j).wait_send()
        for t in range(T):
            reduce_c(t, j).wait_send()
            for dy in (1, 2, 3):
                reduce_y(t, j, dy).wait_send()
                gather_y(t, j, dy, y).wait_send()
            for dy in range(NY):
                gather_c(t, j, dy, c).wait_send()
            if t < T - 1:
                for xx in range(NX):
                    advance(t, j, xx, x).wait_send()


def shards(user_factors, item_factors, tile_blocks, tile_counts, ratings, mask_words):
    dma = pltpu.SemaphoreType.DMA
    vmem = pltpu.VMEM
    space = pl.BlockSpec(memory_space=pl.ANY)
    users, panel = pl.pallas_call(
        kernel,
        out_shape=(
            jax.ShapeDtypeStruct((UB, SIDE, R), BF),
            jax.ShapeDtypeStruct((PIECE, R), F32),
        ),
        in_specs=[
            pl.BlockSpec(memory_space=pltpu.SMEM),
            pl.BlockSpec(memory_space=pltpu.SMEM),
            space,
            pl.BlockSpec(memory_space=pltpu.VMEM),
            space,
            space,
        ],
        out_specs=(space, pl.BlockSpec(memory_space=pltpu.VMEM)),
        scratch_shapes=[
            vmem((UB, SIDE, R), BF),
            vmem((T * K, SIDE, SIDE), BF),
            vmem((T * K, SIDE // 8, SIDE), jnp.int32),
            vmem((T, J, NY, NX, NC, PIECE, W), BF),
            vmem((K + 1, SIDE, SIDE), BF),
            vmem((K + 1, SIDE, SIDE), BF),
            vmem((UB * SIDE, IB * SIDE), BF),
            vmem((IB * SIDE, UB * SIDE), BF),
            vmem((J, NY, NX, NC, PIECE, W), F32),
            vmem((T, J, NY, NX, PIECE, W), BF),
            vmem((T, J, NY, NX, PIECE, W), BF),
            vmem((T, J, 3, NX, PIECE, W), BF),
            vmem((T, J, 3, NX, PIECE, W), BF),
            vmem((T - 1, J, NX, PIECE, W), BF),
            vmem((T - 1, J, NX, NX, PIECE, W), BF),
            vmem((J, PIECE, W), BF),
            vmem((J, PIECE, W), BF),
            dma((3,)),
            dma((T, J)), dma((T, J)),
            dma((T, J, 3)), dma((T, J, 3)),
            dma((T - 1, J, NX)), dma((T - 1, J, NX)),
            dma((J,)), dma((J,)),
            dma((T, J, 3)), dma((T, J, 3)),
            dma((T, J, NY)), dma((T, J, NY)),
            dma((J,)), dma((J,)),
        ],
        compiler_params=pltpu.CompilerParams(
            collective_id=0, has_side_effects=True, vmem_limit_bytes=60 * 1024 * 1024
        ),
    )(
        tile_blocks.reshape(T * K * 2),
        tile_counts.reshape(T),
        user_factors.reshape(UB, SIDE, R),
        item_factors,
        ratings.reshape(T * K, SIDE, SIDE),
        mask_words.reshape(T * K, SIDE // 8, SIDE),
    )
    return users.reshape(UB * SIDE, R), panel


def solution(mesh):
    placed = (
        P(("strata", "shard"), None),
        P(("strata", "shard"), None),
        P("strata", "shard", None, None, None),
        P("strata", "shard", None),
        P("strata", "shard", None, None, None, None),
        P("strata", "shard", None, None, None, None),
    )
    return jax.shard_map(
        shards,
        mesh=mesh,
        in_specs=placed,
        out_specs=(P(("strata", "shard"), None), P(("strata", "shard"), None)),
        check_vma=False,
    )
```

time: 394 us -> 74.6 us (0.19)
  waiting for transfers between devices: 238 us -> 0 us
  blocking collectives: 84.9 us -> 0 us
  Pallas kernels: 0 us -> 69.4 us
  matrix products: 21.6 us -> 0 us
  local copies, waits for them, and re-layouts: 18.3 us -> 4.31 us
  between operations: 14.1 us -> 0.66 us
  other arithmetic: 10.7 us -> 0 us
  starting transfers between devices: 5.43 us -> 0 us
    reduce_scatter x3 -> x0, waiting for transfers between devices: 234 us -> none  [shards(): lax.psum_scatter(grad_item.astype(jnp.bfloat16), 'shard', scatter_dimensi...]
    all_gather x3 -> x0, blocking collectives: 84.9 us -> none  [shards(): lax.all_gather(panel.astype(jnp.bfloat16), 'shard', axis=0, tiled=True)]
    pallas_call x0 -> x1, Pallas kernels: none -> 69.4 us  [shards(): pl.pallas_call(kernel, out_shape=(jax.ShapeDtypeStruct((UB, SIDE, R), BF)...]
    dot_general x15 -> x0, matrix products: 21.6 us -> none  [the longest x3 6.69 us: device_terms(): jnp.einsum('kb,kir->bir', item_hot, item_terms, precision=lax.Precision.H...]
    convert_element_type x9 -> x0, other arithmetic: 8.69 us -> none  [the longest x3 3.86 us: shards(): (factor + step_user * (grad_user - shrinkage * factor)).astype(jnp.bfloat16)]
    gather x6 -> x0, local copies, waits for them, and re-layouts: 5.62 us -> none  [the longest x3 3.78 us: device_terms(): jnp.take(users.reshape(user_count, tile_side, width), blocks[:, 0], axis=0)]
    ppermute x2 -> x0, starting transfers between devices: 5.31 us -> none  [shifted(): return lax.ppermute(x, axis, [(i, (i + by) % peers) for i in range(peers)])]
    dot_general x3 -> x0, local copies, waits for them, and re-layouts: 4.99 us -> none  [device_terms(): jnp.einsum('kb,kur->bur', user_hot, user_terms, precision=lax.Precision.H...]
  transfers between devices with their start and end apart: 5 -> 0, of which waited for: 5 -> 0; matrix products, arithmetic and copies ran while one was open for 5% -> 0% of each run, Pallas kernels for 0% -> 0%
where the time goes in v1:
time: 74.6 us; the launch traced here: 74.4 us
  Pallas kernels  69.4 us (93%)
  local copies, waits for them, and re-layouts  4.31 us (6%)
    pallas_call x1, Pallas kernels, shards(): pl.pallas_call(kernel, out_shape=(jax.ShapeDtypeStruct((UB, SIDE, R), BF)...  69.4 us
    unnamed x7, local copies, waits for them, and re-layouts  3.7 us

profile of v1, /device:TPU:1, one launch (start us, length us, event | category | flops | bytes accessed | tf_op | source)
XLA Modules:
  0.0 74.4 jit_solution(18195234086828220062)
XLA Ops:
  0.6 0.0 copy-start.1
  0.6 0.7 copy-done.1
  1.3 0.1 copy.9
  1.4 0.6 reshape.22.blocks
  2.0 69.4 %shard_map.77 = (bf16[8,128,512]{2,1,0:T(8,128)(2,1)}, f32[32,512]{1,0:T(8,128)}) custom-call(s32[48]{0:T(128)} %reshape.22.blocks, s32[3]{0:T(128)} %bitcast.11, bf16[8,128,512]{2,1,0:T(8,128)(2,1)} %bitcast.8, f32[32,512]{1,0:T(8,128)} %items.1, bf16[24,128,128]{2,1,0:T(8,128)(2,1)} %bitcast.9, s32[24,16,128]{2,1,0:T(8,128)} %bitcast.10), custom_call_target="tpu_custom_call" | custom-call | tf_op jit(solution)/shard_map/pallas_call | solution.py:253
  71.5 0.0 copy-start
  71.5 2.3 %copy.12 = bf16[1024,512]{1,0:T(8,128)(2,1)} copy(bf16[1024,512]{1,0:T(8,128)(2,1)} %bitcast.7) | data formatting | bytes 2097152
  73.8 0.0 copy-done
  73.8 0.6 copy.13
Async XLA Ops:
  0.6 0.7 copy-start.1
  71.5 2.3 %copy-start = (f32[32,512]{1,0:T(8,128)S(1)}, f32[32,512]{1,0:T(8,128)}, u32[]{:S(2)}) copy-start(f32[32,512]{1,0:T(8,128)} %get-tuple-element.9) | copy-start | bytes 196612

commit v2 on v1

v2 whole, which is shorter than its diff:
```python
import jax
import jax.numpy as jnp
from jax import lax
from jax.experimental import pallas as pl
from jax.experimental.pallas import tpu as pltpu
from jax.sharding import PartitionSpec as P

MESH = pl.DeviceIdType.MESH
BF = jnp.bfloat16
F32 = jnp.float32

step_user = 0.05
step_item = 0.004
shrinkage = 0.05

NY, NX, NC = 4, 2, 2
T, K, SIDE, R = 3, 8, 128, 512
J, W = 2, 256
PIECE = 32
UB, IB = 8, 4
N_STRATA = 32
H = 2
PART = PIECE // H
Q = J * H
PEERS = [(2, 1), (1, 1), (3, 1), (2, 0), (0, 1), (1, 0), (3, 0)]


def kernel(
    blocks_in, counts_in, users_in, items_in, ratings_in, words_in,
    users_out, items_out,
    blocks, counts, users, items, ratings, words, panel, err, err_t, dense, dense_t, grads,
    c_out, c_in, y_out, y_in, x_out, x_in, r_out, r_in,
    load_sem, c_send, c_recv, y_send, y_recv, x_send, x_recv, r_send, r_recv,
    g_send, g_recv, p_send, p_recv, i_send, i_recv, k_send, k_recv,
):
    s = lax.axis_index("strata")
    h = lax.axis_index("shard")
    y = h // 4
    x = (h // 2) % 2
    c = h % 2
    after = lax.rem(s + 1, N_STRATA)
    before = lax.rem(s + N_STRATA - 1, N_STRATA)

    def row(dy):
        return lax.rem(y + dy, NY)

    def at(dy, dx, cc):
        return row(dy) * 4 + (1 - x if dx else x) * 2 + cc

    mate = (s, at(0, 0, 1 - c))

    barrier = pltpu.get_barrier_semaphore()
    partners = [mate] + [(s, at(dy, dx, c)) for dy, dx in PEERS]
    partners += [(after, y * 4 + xx * 2 + c) for xx in range(NX)]
    partners += [(before, y * 4 + xx * 2 + c) for xx in range(NX)]
    for partner in partners:
        pl.semaphore_signal(barrier, inc=1, device_id=partner, device_id_type=MESH)

    first_load = pltpu.make_async_copy(items_in, items, load_sem.at[3])
    first_load.start()
    loads = [
        pltpu.make_async_copy(users_in, users, load_sem.at[0]),
        pltpu.make_async_copy(ratings_in, ratings, load_sem.at[1]),
        pltpu.make_async_copy(words_in, words, load_sem.at[2]),
        pltpu.make_async_copy(blocks_in, blocks, load_sem.at[4]),
        pltpu.make_async_copy(counts_in, counts, load_sem.at[5]),
    ]
    for load in loads:
        load.start()

    first_load.wait()
    for j in range(J):
        panel[0, j, y, x, c] = items[:, j * W:(j + 1) * W].astype(BF)

    pl.semaphore_wait(barrier, len(partners))

    def remote(src, dst, send, recv, to):
        return pltpu.make_async_remote_copy(
            src_ref=src, dst_ref=dst, send_sem=send, recv_sem=recv, device_id=to, device_id_type=MESH
        )

    def first_copy(i, yy, xx):
        part = panel.at[0, :, yy, xx, c]
        dy, dx = PEERS[i]
        return remote(part, part, i_send.at[i], i_recv.at[i], (s, at(dy, dx, c)))

    def first_pair(i, yy, xx, cc):
        part = panel.at[0, :, yy, xx, cc]
        return remote(part, part, k_send.at[i], k_recv.at[i], mate)

    def rows_of(q):
        return pl.ds((q % H) * PART, PART)

    def gather_y(t, q, dy, yy):
        part = panel.at[t, q // H, yy, :, c, rows_of(q)]
        return remote(part, part, g_send.at[t - 1, q, dy - 1], g_recv.at[t - 1, q, dy - 1], (s, at(dy, 0, c)))

    def gather_c(t, q, dy, cc):
        part = panel.at[t, q // H, row(4 - dy), :, cc, rows_of(q)]
        return remote(part, part, p_send.at[t - 1, q, dy], p_recv.at[t - 1, q, dy], mate)

    def reduce_c(t, q):
        return remote(c_out.at[t, q], c_in.at[t, q], c_send.at[t, q], c_recv.at[t, q], mate)

    def reduce_y(t, q, dy):
        return remote(
            y_out.at[t, q, dy - 1], y_in.at[t, q, dy - 1], y_send.at[t, q, dy - 1], y_recv.at[t, q, dy - 1],
            (s, at(dy, 0, c)),
        )

    def advance(t, q, xx, slot):
        return remote(
            x_out.at[t, q], x_in.at[t, q, slot], x_send.at[t, q, xx], x_recv.at[t, q, slot],
            (after, y * 4 + xx * 2 + c),
        )

    def reduce_last(j, i):
        dy, dx = PEERS[i]
        return remote(r_out.at[j, i], r_in.at[j, i], r_send.at[j, i], r_recv.at[j, i], (s, at(dy, dx, c)))

    for i in range(len(PEERS)):
        first_copy(i, y, x).start()
    first_pair(len(PEERS), y, x, c).start()
    err[K] = jnp.zeros((SIDE, SIDE), BF)
    err_t[K] = jnp.zeros((SIDE, SIDE), BF)
    for i in reversed(range(len(PEERS))):
        dy, dx = PEERS[i]
        yy, xx = row(4 - dy), (1 - x if dx else x)
        first_copy(i, yy, xx).wait_recv()
        first_pair(i, yy, xx, c).start()
    for load in loads:
        load.wait()
    for i, (dy, dx) in enumerate(PEERS + [(0, 0)]):
        first_pair(i, row(4 - dy), (1 - x if dx else x), 1 - c).wait_recv()

    def slots_of(t):
        cells = [blocks[t, 0, k] * IB + blocks[t, 1, k] for k in range(K)]
        found = []
        for cell in range(UB * IB):
            rank = (cells[0] == cell).astype(jnp.int32) * K
            for k in range(1, K):
                rank = jnp.maximum(rank, (cells[k] == cell).astype(jnp.int32) * (K - k))
            found.append(K - rank)
        return found

    bit = lax.broadcasted_iota(jnp.int32, (16, 8, SIDE), 1)

    def tile_error(t, k):
        a = blocks[t, 0, k]
        b = blocks[t, 1, k]
        live = (k < counts[t]).astype(jnp.int32)
        predicted = jnp.zeros((SIDE, SIDE), F32)
        for j in range(J):
            rows = panel[t, j, b].reshape(SIDE, W)
            predicted += lax.dot_general(
                users[a, :, j * W:(j + 1) * W], rows, (((1,), (1,)), ((), ())), preferred_element_type=F32
            )
        mask = jnp.bitwise_and(jnp.right_shift(words[t * K + k][:, None, :], bit), live).reshape(SIDE, SIDE)
        error = jnp.where(mask != 0, ratings[t * K + k].astype(F32) - predicted, 0.0)
        err[k] = error.astype(BF)
        err_t[k] = error.T.astype(BF)

    def update_users(t, j):
        columns = slice(j * W, (j + 1) * W)
        grad = jnp.dot(dense[...], panel[t, j].reshape(IB * SIDE, W), preferred_element_type=F32)
        grad = grad.reshape(UB, SIDE, W)
        factor = users[:, :, columns].astype(F32)
        users[:, :, columns] = (factor + step_user * (grad - shrinkage * factor)).astype(BF)

    def paired(t, q, yy, xx=slice(None)):
        mine = grads[q // H, yy, xx, c, (q % H) * PART:(q % H + 1) * PART]
        return mine + c_in[t, q, yy, xx].astype(F32)

    for t in range(T):
        for k in range(K):
            tile_error(t, k)
        slots = slots_of(t)
        for b in range(IB):
            for a in range(UB):
                dense_t[b * SIDE:(b + 1) * SIDE, a * SIDE:(a + 1) * SIDE] = err_t[slots[a * IB + b]]
        for j in range(J):
            grads[j] = jnp.dot(
                dense_t[...], users[:, :, j * W:(j + 1) * W].reshape(UB * SIDE, W), preferred_element_type=F32
            ).reshape(NY, NX, NC, PIECE, W)
            for q in range(j * H, (j + 1) * H):
                c_out[t, q] = grads[j, :, :, 1 - c, (q % H) * PART:(q % H + 1) * PART].astype(BF)
                reduce_c(t, q).start()
        for b in range(IB):
            for a in range(UB):
                dense[a * SIDE:(a + 1) * SIDE, b * SIDE:(b + 1) * SIDE] = err[slots[a * IB + b]]
        if t < T - 1:
            for q in range(Q):
                reduce_c(t, q).wait_recv()
                for dy in (2, 1, 3):
                    y_out[t, q, dy - 1] = paired(t, q, row(dy)).astype(BF)
                    reduce_y(t, q, dy).start()
            for j in range(J):
                update_users(t, j)
            for q in range(Q):
                total = paired(t, q, y)
                for dy in (1, 3, 2):
                    reduce_y(t, q, dy).wait_recv()
                    total += y_in[t, q, dy - 1].astype(F32)
                mine = panel[t, q // H, y, :, c, (q % H) * PART:(q % H + 1) * PART].astype(F32)
                half = step_item * total + (0.5 * (1.0 - step_item * shrinkage)) * mine
                x_out[t, q] = half.astype(BF)
                for xx in range(NX):
                    advance(t, q, xx, x).start()
            for q in range(Q):
                for xx in range(NX):
                    advance(t, q, xx, xx).wait_recv()
                both = x_in[t, q, 0].astype(F32) + x_in[t, q, 1].astype(F32)
                panel[t + 1, q // H, y, :, c, (q % H) * PART:(q % H + 1) * PART] = both.astype(BF)
                for dy in (2, 1, 3):
                    gather_y(t + 1, q, dy, y).start()
                gather_c(t + 1, q, 0, c).start()
            for q in range(Q):
                for dy in (1, 3, 2):
                    gather_y(t + 1, q, dy, row(4 - dy)).wait_recv()
                    gather_c(t + 1, q, dy, c).start()
            for q in range(Q):
                for dy in range(NY):
                    gather_c(t + 1, q, dy, 1 - c).wait_recv()
        else:
            for j in range(J):
                for q in range(j * H, (j + 1) * H):
                    reduce_c(t, q).wait_recv()
                for i, (dy, dx) in enumerate(PEERS):
                    for q in range(j * H, (j + 1) * H):
                        part = paired(t, q, row(dy), 1 - x if dx else x)
                        r_out[j, i, (q % H) * PART:(q % H + 1) * PART] = part.astype(BF)
                    reduce_last(j, i).start()
            for j in range(J):
                update_users(t, j)
            out = pltpu.make_async_copy(users, users_out, load_sem.at[0])
            out.start()
            for j in range(J):
                own = [paired(t, q, y, x) for q in range(j * H, (j + 1) * H)]
                total = jnp.concatenate(own, axis=0)
                for i in reversed(range(len(PEERS))):
                    reduce_last(j, i).wait_recv()
                    total += r_in[j, i].astype(F32)
                mine = panel[t, j, y, x, c].astype(F32)
                items[:, j * W:(j + 1) * W] = mine + step_item * (total - shrinkage * mine)
            last = pltpu.make_async_copy(items, items_out, load_sem.at[1])
            last.start()

    for i in range(len(PEERS)):
        first_copy(i, y, x).wait_send()
        first_pair(i, y, x, c).wait_send()
        for j in range(J):
            reduce_last(j, i).wait_send()
    first_pair(len(PEERS), y, x, c).wait_send()
    for q in range(Q):
        for t in range(T):
            reduce_c(t, q).wait_send()
        for t in range(T - 1):
            for dy in (1, 2, 3):
                reduce_y(t, q, dy).wait_send()
                gather_y(t + 1, q, dy, y).wait_send()
            for dy in range(NY):
                gather_c(t + 1, q, dy, c).wait_send()
            for xx in range(NX):
                advance(t, q, xx, x).wait_send()
    out.wait()
    last.wait()


def shards(user_factors, item_factors, tile_blocks, tile_counts, ratings, mask_words):
    dma = pltpu.SemaphoreType.DMA
    vmem = pltpu.VMEM
    space = pl.BlockSpec(memory_space=pl.ANY)
    fixed = pl.BlockSpec(memory_space=pltpu.HBM)
    n = len(PEERS)

    def far(a):
        return pltpu.with_memory_space_constraint(a, pltpu.HBM)

    users, panel = pl.pallas_call(
        kernel,
        out_shape=(
            jax.ShapeDtypeStruct((UB, SIDE, R), BF),
            jax.ShapeDtypeStruct((PIECE, R), F32),
        ),
        in_specs=[
            fixed,
            fixed,
            fixed,
            fixed,
            fixed,
            fixed,
        ],
        out_specs=(space, space),
        scratch_shapes=[
            pltpu.SMEM((T, 2, K), jnp.int32),
            pltpu.SMEM((T,), jnp.int32),
            vmem((UB, SIDE, R), BF),
            vmem((PIECE, R), F32),
            vmem((T * K, SIDE, SIDE), BF),
            vmem((T * K, SIDE // 8, SIDE), jnp.int32),
            vmem((T, J, NY, NX, NC, PIECE, W), BF),
            vmem((K + 1, SIDE, SIDE), BF),
            vmem((K + 1, SIDE, SIDE), BF),
            vmem((UB * SIDE, IB * SIDE), BF),
            vmem((IB * SIDE, UB * SIDE), BF),
            vmem((J, NY, NX, NC, PIECE, W), F32),
            vmem((T, Q, NY, NX, PART, W), BF),
            vmem((T, Q, NY, NX, PART, W), BF),
            vmem((T - 1, Q, 3, NX, PART, W), BF),
            vmem((T - 1, Q, 3, NX, PART, W), BF),
            vmem((T - 1, Q, NX, PART, W), BF),
            vmem((T - 1, Q, NX, NX, PART, W), BF),
            vmem((J, n, PIECE, W), BF),
            vmem((J, n, PIECE, W), BF),
            dma((6,)),
            dma((T, Q)), dma((T, Q)),
            dma((T - 1, Q, 3)), dma((T - 1, Q, 3)),
            dma((T - 1, Q, NX)), dma((T - 1, Q, NX)),
            dma((J, n)), dma((J, n)),
            dma((T - 1, Q, 3)), dma((T - 1, Q, 3)),
            dma((T - 1, Q, NY)), dma((T - 1, Q, NY)),
            dma((n,)), dma((n,)),
            dma((n + 1,)), dma((n + 1,)),
        ],
        compiler_params=pltpu.CompilerParams(
            collective_id=0, has_side_effects=True, vmem_limit_bytes=24 * 1024 * 1024
        ),
    )(
        far(tile_blocks.reshape(T, K, 2).transpose(0, 2, 1)),
        far(tile_counts.reshape(T)),
        far(user_factors.reshape(UB, SIDE, R)),
        far(item_factors),
        far(ratings.reshape(T * K, SIDE, SIDE)),
        far(mask_words.reshape(T * K, SIDE // 8, SIDE)),
    )
    return users.reshape(UB * SIDE, R), panel


def solution(mesh):
    placed = (
        P(("strata", "shard"), None),
        P(("strata", "shard"), None),
        P("strata", "shard", None, None, None),
        P("strata", "shard", None),
        P("strata", "shard", None, None, None, None),
        P("strata", "shard", None, None, None, None),
    )
    return jax.shard_map(
        shards,
        mesh=mesh,
        in_specs=placed,
        out_specs=(P(("strata", "shard"), None), P(("strata", "shard"), None)),
        check_vma=False,
    )
```

time: 74.6 us -> 66 us (0.88)
  Pallas kernels: 69.4 us -> 63.6 us
  local copies, waits for them, and re-layouts: 4.31 us -> 1.6 us
    pallas_call x1, Pallas kernels: 69.4 us -> 63.6 us  [shards(): pl.pallas_call(kernel, out_shape=(jax.ShapeDtypeStruct((UB, SIDE, R), BF)...]
    unnamed x7 -> x2, local copies, waits for them, and re-layouts: 3.7 us -> 1.6 us
where the time goes in v2:
time: 66 us; the launch traced here: 65.9 us
  Pallas kernels  63.6 us (96%)
  local copies, waits for them, and re-layouts  1.6 us (2%)
    pallas_call x1, Pallas kernels, shards(): pl.pallas_call(kernel, out_shape=(jax.ShapeDtypeStruct((UB, SIDE, R), BF)...  63.6 us
    unnamed x2, local copies, waits for them, and re-layouts  1.6 us

profile of v2, /device:TPU:1, one launch (start us, length us, event | category | flops | bytes accessed | tf_op | source)
XLA Modules:
  0.0 65.9 jit_solution(824186460000556774)
XLA Ops:
  0.6 63.6 %shard_map.77 = (bf16[8,128,512]{2,1,0:T(8,128)(2,1)S(1)}, f32[32,512]{1,0:T(8,128)S(1)}) custom-call(s32[3,2,8]{2,1,0:T(2,128)} %bitcast.12, s32[3]{0:T(128)} %bitcast.13, bf16[8,128,512]{2,1,0:T(8,128)(2,1)} %bitcast.9, f32[32,512]{1,0:T(8,128)} %items_in.1, bf16[24,128,128]{2,1,0:T(8,128)(2,1)} %bitcast.10, s32[24,16,128]{2,1,0:T(8,128)} %bitcast.11), custom_call_target="tpu_custom_call" | custom-call | tf_op jit(solution)/shard_map/pallas_call | solution.py:279
  64.3 1.0 %copy.10 = bf16[1024,512]{1,0:T(8,128)(2,1)} copy(bf16[1024,512]{1,0:T(8,128)(2,1)S(1)} %bitcast.8) | data formatting | bytes 2097152
  65.3 0.6 copy.11

commit v3 on v2

v3 whole, which is shorter than its diff:
```python
import jax
import jax.numpy as jnp
from jax import lax
from jax.experimental import pallas as pl
from jax.experimental.pallas import tpu as pltpu
from jax.sharding import PartitionSpec as P

MESH = pl.DeviceIdType.MESH
BF = jnp.bfloat16
F32 = jnp.float32

step_user = 0.05
step_item = 0.004
shrinkage = 0.05

NY, NX, NC = 4, 2, 2
T, K, SIDE, R = 3, 8, 128, 512
J, W = 2, 256
PIECE = 32
UB, IB = 8, 4
N_STRATA = 32
H = 2
PART = PIECE // H
Q = J * H
MARK = 1e30
LIMIT = 1e20
PEERS = [(2, 1), (1, 1), (3, 1), (2, 0), (0, 1), (1, 0), (3, 0)]


def kernel(
    blocks_in, counts_in, users_in, items_in, ratings_in, words_in,
    users_out, items_out,
    blocks, counts, users, items, ratings, words, marked, panel0, panels, predicted, err_t, dense_t, grads,
    u_own, u_out, u_in, y_out, y_in, x_out, x_in, r_out, r_in,
    load_sem, pair_send, pair_recv, u_send, u_recv, n_send, n_recv, y_send, y_recv, x_send, x_recv,
    r_send, r_recv, g_send, g_recv, i_send, i_recv,
):
    s = lax.axis_index("strata")
    h = lax.axis_index("shard")
    y = h // 4
    x = (h // 2) % 2
    c = h % 2
    after = lax.rem(s + 1, N_STRATA)
    before = lax.rem(s + N_STRATA - 1, N_STRATA)

    def row(dy):
        return lax.rem(y + dy, NY)

    def at(dy, dx, cc):
        return row(dy) * 4 + (1 - x if dx else x) * 2 + cc

    mate = (s, at(0, 0, 1 - c))

    barrier = pltpu.get_barrier_semaphore()
    partners = [mate] + [(s, at(dy, dx, c)) for dy, dx in PEERS]
    partners += [(after, y * 4 + xx * 2 + c) for xx in range(NX)]
    partners += [(before, y * 4 + xx * 2 + c) for xx in range(NX)]
    for partner in partners:
        pl.semaphore_signal(barrier, inc=1, device_id=partner, device_id_type=MESH)

    first_load = pltpu.make_async_copy(items_in, items, load_sem.at[0])
    first_load.start()
    pairs = [(blocks_in, blocks), (counts_in, counts), (ratings_in, ratings), (words_in, words), (users_in, users)]
    loads = [pltpu.make_async_copy(src, dst.at[0], load_sem.at[n + 1]) for n, (src, dst) in enumerate(pairs)]
    for load in loads:
        load.start()

    first_load.wait()
    for j in range(J):
        panel0[j, y, x] = items[:, j * W:(j + 1) * W].astype(BF)

    pl.semaphore_wait(barrier, len(partners))

    def remote(src, dst, send, recv, to):
        return pltpu.make_async_remote_copy(
            src_ref=src, dst_ref=dst, send_sem=send, recv_sem=recv, device_id=to, device_id_type=MESH
        )

    def panel_at(t, j, *index):
        return panels[t - 1][j][index] if t else panel0[(j, *index)]

    def first_copy(i, yy, xx):
        part = panel0.at[:, yy, xx]
        dy, dx = PEERS[i]
        return remote(part, part, i_send.at[i], i_recv.at[i], (s, at(dy, dx, c)))

    def share(n):
        src, dst = pairs[n]
        return remote(src, dst.at[1], pair_send.at[n], pair_recv.at[n], mate)

    def rows_of(q):
        return pl.ds((q % H) * PART, PART)

    def gather_y(t, q, dy, yy):
        part = panels[t - 1][q // H].at[yy, :, rows_of(q)]
        return remote(part, part, g_send.at[t - 1, q, dy - 1], g_recv.at[t - 1, q, dy - 1], (s, at(dy, 0, c)))

    def reduce_y(t, q, dy):
        return remote(
            y_out.at[t, q, dy - 1], y_in.at[t, q, dy - 1], y_send.at[t, q, dy - 1], y_recv.at[t, q, dy - 1],
            (s, at(dy, 0, c)),
        )

    def advance(t, q, xx, slot):
        return remote(
            x_out.at[t, q], x_in.at[t, q, slot], x_send.at[t, q, xx], x_recv.at[t, q, slot],
            (after, y * 4 + xx * 2 + c),
        )

    def reduce_last(j, i):
        dy, dx = PEERS[i]
        return remote(r_out.at[j, i], r_in.at[j, i], r_send.at[j, i], r_recv.at[j, i], (s, at(dy, dx, c)))

    def user_grads(t):
        return remote(u_out.at[t], u_in.at[t], u_send.at[t], u_recv.at[t], mate)

    def new_users(t):
        return remote(users.at[0], users.at[1], n_send.at[t], n_recv.at[t], mate)

    bit = lax.broadcasted_iota(jnp.int32, (16, 8, SIDE), 1)

    def mark(t, cc):
        for k in range(K):
            live = (k < counts[cc, t]).astype(jnp.int32)
            mask = jnp.bitwise_and(jnp.right_shift(words[cc, t * K + k][:, None, :], bit), live).reshape(SIDE, SIDE)
            rate = jnp.where(mask != 0, ratings[cc, t * K + k].astype(F32), MARK)
            marked[cc * K + k] = rate.T.astype(BF).reshape(NX, NC, PIECE, SIDE)

    def slots_of(t):
        found = []
        for cc in range(NC):
            cells = [blocks[cc, t, 0, k] * IB + blocks[cc, t, 1, k] for k in range(K)]
            for cell in range(UB * IB):
                rank = (cells[0] == cell).astype(jnp.int32) * (2 * K - cc * K)
                for k in range(1, K):
                    rank = jnp.maximum(rank, (cells[k] == cell).astype(jnp.int32) * (2 * K - cc * K - k))
                found.append(2 * K - rank)
        return found

    def product(t, j, cc, k):
        rows = panel_at(t, j, blocks[cc, t, 1, k]).reshape(NX * PIECE, W)
        return lax.dot_general(
            rows, users[cc, blocks[cc, t, 0, k], :, j * W:(j + 1) * W], (((1,), (1,)), ((), ())),
            preferred_element_type=F32,
        )

    def predict_first(t):
        for cc in range(NC):
            for k in range(K):
                predicted[cc * K + k] = product(t, 0, cc, k)

    def errors(t):
        for cc in range(NC):
            for k in range(K):
                value = predicted[cc * K + k] + product(t, 1, cc, k)
                rate = marked[cc * K + k, :, c].reshape(NX * PIECE, SIDE).astype(F32)
                err_t[cc * K + k] = jnp.where(rate < LIMIT, rate - value, 0.0).astype(BF)

    def user_grad(t, cc, j):
        return lax.dot_general(
            dense_t[:, cc * UB * SIDE:(cc + 1) * UB * SIDE], panel_at(t, j, slice(None)).reshape(NY * NX * PIECE, W),
            (((0,), (0,)), ((), ())), preferred_element_type=F32,
        ).reshape(UB, SIDE, W)

    def columns(j):
        return slice(j * W, (j + 1) * W)

    def send_user_grads(t):
        for j in range(J):
            u_out[t, :, :, columns(j)] = user_grad(t, 1, j).astype(BF)
        user_grads(t).start()
        for j in range(J):
            u_own[:, :, columns(j)] = user_grad(t, 0, j)

    def update_users(t):
        user_grads(t).wait_recv()
        if t > 0:
            new_users(t - 1).wait_send()
        for j in range(J):
            grad = u_own[:, :, columns(j)] + u_in[t, :, :, columns(j)].astype(F32)
            factor = users[0, :, :, columns(j)].astype(F32)
            users[0, :, :, columns(j)] = (factor + step_user * (grad - shrinkage * factor)).astype(BF)

    for i in range(len(PEERS)):
        first_copy(i, y, x).start()
    for n in range(len(pairs)):
        share(n).start()
    err_t[2 * K] = jnp.zeros((NX * PIECE, SIDE), BF)
    for load in loads:
        load.wait()
    mark(0, 0)
    for n in range(len(pairs)):
        share(n).wait_recv()
    mark(0, 1)
    slots = slots_of(0)
    for i, (dy, dx) in enumerate(PEERS):
        first_copy(i, row(4 - dy), (1 - x if dx else x)).wait_recv()
    predict_first(0)

    for t in range(T):
        errors(t)
        for cc in range(NC):
            for b in range(IB):
                for a in range(UB):
                    lanes = slice((cc * UB + a) * SIDE, (cc * UB + a + 1) * SIDE)
                    dense_t[b * NX * PIECE:(b + 1) * NX * PIECE, lanes] = err_t[slots[(cc * UB + a) * IB + b]]
        for j in range(J):
            grads[j] = jnp.dot(
                dense_t[...], users[:, :, :, columns(j)].reshape(NC * UB * SIDE, W), preferred_element_type=F32
            ).reshape(NY, NX, PIECE, W)
            if t < T - 1:
                for q in range(j * H, (j + 1) * H):
                    for dy in (2, 1, 3):
                        y_out[t, q, dy - 1] = grads[j, row(dy), :, (q % H) * PART:(q % H + 1) * PART].astype(BF)
                        reduce_y(t, q, dy).start()
            else:
                for i, (dy, dx) in enumerate(PEERS):
                    r_out[j, i] = grads[j, row(dy), 1 - x if dx else x].astype(BF)
                    reduce_last(j, i).start()
        send_user_grads(t)
        if t < T - 1:
            for q in range(Q):
                total = grads[q // H, y, :, (q % H) * PART:(q % H + 1) * PART]
                for dy in (1, 3, 2):
                    reduce_y(t, q, dy).wait_recv()
                    total += y_in[t, q, dy - 1].astype(F32)
                mine = panel_at(t, q // H, y, slice(None), slice((q % H) * PART, (q % H + 1) * PART)).astype(F32)
                half = step_item * total + (0.5 * (1.0 - step_item * shrinkage)) * mine
                x_out[t, q] = half.astype(BF)
                for xx in range(NX):
                    advance(t, q, xx, x).start()
            update_users(t)
            new_users(t).start()
            for q in range(Q):
                for xx in range(NX):
                    advance(t, q, xx, xx).wait_recv()
                both = x_in[t, q, 0].astype(F32) + x_in[t, q, 1].astype(F32)
                panels[t][q // H][y, :, (q % H) * PART:(q % H + 1) * PART] = both.astype(BF)
                for dy in (2, 1, 3):
                    gather_y(t + 1, q, dy, y).start()
            for cc in range(NC):
                mark(t + 1, cc)
            slots = slots_of(t + 1)
            new_users(t).wait_recv()
            for q in range(H):
                for dy in (1, 3, 2):
                    gather_y(t + 1, q, dy, row(4 - dy)).wait_recv()
            predict_first(t + 1)
            for q in range(H, Q):
                for dy in (1, 3, 2):
                    gather_y(t + 1, q, dy, row(4 - dy)).wait_recv()
        else:
            update_users(t)
            out = pltpu.make_async_copy(users.at[0], users_out, load_sem.at[0])
            out.start()
            for j in range(J):
                total = grads[j, y, x]
                for i in reversed(range(len(PEERS))):
                    reduce_last(j, i).wait_recv()
                    total += r_in[j, i].astype(F32)
                mine = panel_at(t, j, y, x).astype(F32)
                items[:, columns(j)] = mine + step_item * (total - shrinkage * mine)
            last = pltpu.make_async_copy(items, items_out, load_sem.at[1])
            last.start()

    for n in range(len(pairs)):
        share(n).wait_send()
    for i in range(len(PEERS)):
        first_copy(i, y, x).wait_send()
        for j in range(J):
            reduce_last(j, i).wait_send()
    for t in range(T):
        user_grads(t).wait_send()
    for t in range(T - 1):
        for q in range(Q):
            for dy in (1, 2, 3):
                reduce_y(t, q, dy).wait_send()
                gather_y(t + 1, q, dy, y).wait_send()
            for xx in range(NX):
                advance(t, q, xx, x).wait_send()
    out.wait()
    last.wait()


def shards(user_factors, item_factors, tile_blocks, tile_counts, ratings, mask_words):
    dma = pltpu.SemaphoreType.DMA
    vmem = pltpu.VMEM
    space = pl.BlockSpec(memory_space=pl.ANY)
    n = len(PEERS)

    def far(a):
        return pltpu.with_memory_space_constraint(a, pltpu.HBM)

    users, panel = pl.pallas_call(
        kernel,
        out_shape=(
            jax.ShapeDtypeStruct((UB, SIDE, R), BF),
            jax.ShapeDtypeStruct((PIECE, R), F32),
        ),
        in_specs=[pl.BlockSpec(memory_space=pltpu.HBM)] * 6,
        out_specs=(space, space),
        scratch_shapes=[
            pltpu.SMEM((NC, T, 2, K), jnp.int32),
            pltpu.SMEM((NC, T), jnp.int32),
            vmem((NC, UB, SIDE, R), BF),
            vmem((PIECE, R), F32),
            vmem((NC, T * K, SIDE, SIDE), BF),
            vmem((NC, T * K, SIDE // 8, SIDE), jnp.int32),
            vmem((NC * K, NX, NC, PIECE, SIDE), BF),
            vmem((J, NY, NX, PIECE, W), BF),
            [[vmem((NY, NX, PIECE, W), BF) for j in range(J)] for t in range(T - 1)],
            vmem((NC * K, NX * PIECE, SIDE), F32),
            vmem((NC * K + 1, NX * PIECE, SIDE), BF),
            vmem((NY * NX * PIECE, NC * UB * SIDE), BF),
            vmem((J, NY, NX, PIECE, W), F32),
            vmem((UB, SIDE, R), F32),
            vmem((T, UB, SIDE, R), BF),
            vmem((T, UB, SIDE, R), BF),
            vmem((T - 1, Q, 3, NX, PART, W), BF),
            vmem((T - 1, Q, 3, NX, PART, W), BF),
            vmem((T - 1, Q, NX, PART, W), BF),
            vmem((T - 1, Q, NX, NX, PART, W), BF),
            vmem((J, n, PIECE, W), BF),
            vmem((J, n, PIECE, W), BF),
            dma((6,)),
            dma((5,)), dma((5,)),
            dma((T,)), dma((T,)),
            dma((T - 1,)), dma((T - 1,)),
            dma((T - 1, Q, 3)), dma((T - 1, Q, 3)),
            dma((T - 1, Q, NX)), dma((T - 1, Q, NX)),
            dma((J, n)), dma((J, n)),
            dma((T - 1, Q, 3)), dma((T - 1, Q, 3)),
            dma((n,)), dma((n,)),
        ],
        compiler_params=pltpu.CompilerParams(
            collective_id=0, has_side_effects=True, vmem_limit_bytes=36 * 1024 * 1024
        ),
    )(
        far(tile_blocks.reshape(T, K, 2).transpose(0, 2, 1)),
        far(tile_counts.reshape(T)),
        far(user_factors.reshape(UB, SIDE, R)),
        far(item_factors),
        far(ratings.reshape(T * K, SIDE, SIDE)),
        far(mask_words.reshape(T * K, SIDE // 8, SIDE)),
    )
    return users.reshape(UB * SIDE, R), panel


def solution(mesh):
    placed = (
        P(("strata", "shard"), None),
        P(("strata", "shard"), None),
        P("strata", "shard", None, None, None),
        P("strata", "shard", None),
        P("strata", "shard", None, None, None, None),
        P("strata", "shard", None, None, None, None),
    )
    return jax.shard_map(
        shards,
        mesh=mesh,
        in_specs=placed,
        out_specs=(P(("strata", "shard"), None), P(("strata", "shard"), None)),
        check_vma=False,
    )
```

time: 66 us -> 58 us (0.88)
  Pallas kernels: 63.6 us -> 55.7 us
    pallas_call x1, Pallas kernels: 63.6 us -> 55.7 us  [shards(): pl.pallas_call(kernel, out_shape=(jax.ShapeDtypeStruct((UB, SIDE, R), BF)...]
where the time goes in v3:
time: 58 us; the launch traced here: 57.9 us
  Pallas kernels  55.7 us (96%)
  local copies, waits for them, and re-layouts  1.6 us (3%)
  between operations  0.64 us (1%)
    pallas_call x1, Pallas kernels, shards(): pl.pallas_call(kernel, out_shape=(jax.ShapeDtypeStruct((UB, SIDE, R), BF)...  55.7 us
    unnamed x2, local copies, waits for them, and re-layouts  1.6 us

profile of v3, /device:TPU:1, one launch (start us, length us, event | category | flops | bytes accessed | tf_op | source)
XLA Modules:
  0.0 57.9 jit_solution(16680672578060801327)
XLA Ops:
  0.6 55.7 %shard_map.77 = (bf16[8,128,512]{2,1,0:T(8,128)(2,1)S(1)}, f32[32,512]{1,0:T(8,128)S(1)}) custom-call(s32[3,2,8]{2,1,0:T(2,128)} %bitcast.12, s32[3]{0:T(128)} %bitcast.13, bf16[8,128,512]{2,1,0:T(8,128)(2,1)} %bitcast.9, f32[32,512]{1,0:T(8,128)} %items_in.1, bf16[24,128,128]{2,1,0:T(8,128)(2,1)} %bitcast.10, s32[24,16,128]{2,1,0:T(8,128)} %bitcast.11), custom_call_target="tpu_custom_call" | custom-call | tf_op jit(solution)/shard_map/pallas_call | solution.py:294
  56.3 1.0 %copy.10 = bf16[1024,512]{1,0:T(8,128)(2,1)} copy(bf16[1024,512]{1,0:T(8,128)(2,1)S(1)} %bitcast.8) | data formatting | bytes 2097152
  57.3 0.6 %copy.11 = f32[32,512]{1,0:T(8,128)} copy(f32[32,512]{1,0:T(8,128)S(1)} %get-tuple-element.9) | data formatting | bytes 131072

commit v4 on v3

--- a/solution.py
+++ b/solution.py
@@ -30,7 +30,7 @@
 def kernel(
     blocks_in, counts_in, users_in, items_in, ratings_in, words_in,
     users_out, items_out,
-    blocks, counts, users, items, ratings, words, marked, panel0, panels, predicted, err_t, dense_t, grads,
+    blocks, counts, users, items, ratings, words, marked, rates, panel0, panels, remaining, dense_t, grads,
     u_own, u_out, u_in, y_out, y_in, x_out, x_in, r_out, r_in,
     load_sem, pair_send, pair_recv, u_send, u_recv, n_send, n_recv, y_send, y_recv, x_send, x_recv,
     r_send, r_recv, g_send, g_recv, i_send, i_recv,
@@ -117,6 +117,9 @@
     def new_users(t):
         return remote(users.at[0], users.at[1], n_send.at[t], n_recv.at[t], mate)
 
+    def columns(j):
+        return slice(j * W, (j + 1) * W)
+
     bit = lax.broadcasted_iota(jnp.int32, (16, 8, SIDE), 1)
 
     def mark(t, cc):
@@ -137,24 +140,34 @@
                 found.append(2 * K - rank)
         return found
 
-    def product(t, j, cc, k):
-        rows = panel_at(t, j, blocks[cc, t, 1, k]).reshape(NX * PIECE, W)
+    def place(t):
+        slots = slots_of(t)
+        for cc in range(NC):
+            for b in range(IB):
+                for a in range(UB):
+                    lanes = slice((cc * UB + a) * SIDE, (cc * UB + a + 1) * SIDE)
+                    tile = marked[slots[(cc * UB + a) * IB + b], :, c]
+                    rates[b * NX * PIECE:(b + 1) * NX * PIECE, lanes] = tile.reshape(NX * PIECE, SIDE)
+
+    def product(t, j, n):
+        cc, a = divmod(2 * n, UB)
         return lax.dot_general(
-            rows, users[cc, blocks[cc, t, 0, k], :, j * W:(j + 1) * W], (((1,), (1,)), ((), ())),
-            preferred_element_type=F32,
+            panel_at(t, j, slice(None)).reshape(NY * NX * PIECE, W),
+            users[cc, a:a + 2, :, columns(j)].reshape(2 * SIDE, W),
+            (((1,), (1,)), ((), ())), preferred_element_type=F32,
         )
 
+    def group(n):
+        return slice(n * 2 * SIDE, (n + 1) * 2 * SIDE)
+
     def predict_first(t):
-        for cc in range(NC):
-            for k in range(K):
-                predicted[cc * K + k] = product(t, 0, cc, k)
+        for n in range(UB):
+            remaining[n] = rates[:, group(n)].astype(F32) - product(t, 0, n)
 
     def errors(t):
-        for cc in range(NC):
-            for k in range(K):
-                value = predicted[cc * K + k] + product(t, 1, cc, k)
-                rate = marked[cc * K + k, :, c].reshape(NX * PIECE, SIDE).astype(F32)
-                err_t[cc * K + k] = jnp.where(rate < LIMIT, rate - value, 0.0).astype(BF)
+        for n in range(UB):
+            rest = remaining[n]
+            dense_t[:, group(n)] = jnp.where(rest < LIMIT, rest - product(t, 1, n), 0.0).astype(BF)
 
     def user_grad(t, cc, j):
         return lax.dot_general(
@@ -162,9 +175,6 @@
             (((0,), (0,)), ((), ())), preferred_element_type=F32,
         ).reshape(UB, SIDE, W)
 
-    def columns(j):
-        return slice(j * W, (j + 1) * W)
-
     def send_user_grads(t):
         for j in range(J):
             u_out[t, :, :, columns(j)] = user_grad(t, 1, j).astype(BF)
@@ -185,25 +195,20 @@
         first_copy(i, y, x).start()
     for n in range(len(pairs)):
         share(n).start()
-    err_t[2 * K] = jnp.zeros((NX * PIECE, SIDE), BF)
+    marked[2 * K] = jnp.full((NX, NC, PIECE, SIDE), MARK, BF)
     for load in loads:
         load.wait()
     mark(0, 0)
     for n in range(len(pairs)):
         share(n).wait_recv()
     mark(0, 1)
-    slots = slots_of(0)
+    place(0)
     for i, (dy, dx) in enumerate(PEERS):
         first_copy(i, row(4 - dy), (1 - x if dx else x)).wait_recv()
     predict_first(0)
 
     for t in range(T):
         errors(t)
-        for cc in range(NC):
-            for b in range(IB):
-                for a in range(UB):
-                    lanes = slice((cc * UB + a) * SIDE, (cc * UB + a + 1) * SIDE)
-                    dense_t[b * NX * PIECE:(b + 1) * NX * PIECE, lanes] = err_t[slots[(cc * UB + a) * IB + b]]
         for j in range(J):
             grads[j] = jnp.dot(
                 dense_t[...], users[:, :, :, columns(j)].reshape(NC * UB * SIDE, W), preferred_element_type=F32
@@ -240,7 +245,7 @@
                     gather_y(t + 1, q, dy, y).start()
             for cc in range(NC):
                 mark(t + 1, cc)
-            slots = slots_of(t + 1)
+            place(t + 1)
             new_users(t).wait_recv()
             for q in range(H):
                 for dy in (1, 3, 2):
@@ -282,6 +287,17 @@
     last.wait()
 
 
+def store(users_in, items_in, users_out, items_out, sem):
+    copies = [
+        pltpu.make_async_copy(users_in, users_out, sem.at[0]),
+        pltpu.make_async_copy(items_in, items_out, sem.at[1]),
+    ]
+    for copy in copies:
+        copy.start()
+    for copy in copies:
+        copy.wait()
+
+
 def shards(user_factors, item_factors, tile_blocks, tile_counts, ratings, mask_words):
     dma = pltpu.SemaphoreType.DMA
     vmem = pltpu.VMEM
@@ -306,11 +322,11 @@
             vmem((PIECE, R), F32),
             vmem((NC, T * K, SIDE, SIDE), BF),
             vmem((NC, T * K, SIDE // 8, SIDE), jnp.int32),
-            vmem((NC * K, NX, NC, PIECE, SIDE), BF),
+            vmem((NC * K + 1, NX, NC, PIECE, SIDE), BF),
+            vmem((NY * NX * PIECE, NC * UB * SIDE), BF),
             vmem((J, NY, NX, PIECE, W), BF),
             [[vmem((NY, NX, PIECE, W), BF) for j in range(J)] for t in range(T - 1)],
-            vmem((NC * K, NX * PIECE, SIDE), F32),
-            vmem((NC * K + 1, NX * PIECE, SIDE), BF),
+            vmem((UB, NY * NX * PIECE, 2 * SIDE), F32),
             vmem((NY * NX * PIECE, NC * UB * SIDE), BF),
             vmem((J, NY, NX, PIECE, W), F32),
             vmem((UB, SIDE, R), F32),
@@ -343,6 +359,17 @@
         far(ratings.reshape(T * K, SIDE, SIDE)),
         far(mask_words.reshape(T * K, SIDE // 8, SIDE)),
     )
+    users, panel = pl.pallas_call(
+        store,
+        out_shape=(
+            jax.ShapeDtypeStruct((UB, SIDE, R), BF),
+            jax.ShapeDtypeStruct((PIECE, R), F32),
+        ),
+        in_specs=[space] * 2,
+        out_specs=(pl.BlockSpec(memory_space=pltpu.HBM),) * 2,
+        scratch_shapes=[dma((2,))],
+        compiler_params=pltpu.CompilerParams(vmem_limit_bytes=1024 * 1024),
+    )(users, panel)
     return users.reshape(UB * SIDE, R), panel
 
 

time: 58 us -> 57 us (0.983)
  local copies, waits for them, and re-layouts: 1.6 us -> 0 us
    unnamed x2 -> x0, local copies, waits for them, and re-layouts: 1.6 us -> none
    pallas_call x0 -> x1, Pallas kernels: none -> 0.99 us  [shards(): pl.pallas_call(store, out_shape=(jax.ShapeDtypeStruct((UB, SIDE, R), BF),...]
where the time goes in v4:
time: 57 us; the launch traced here: 56.9 us
  Pallas kernels  56.2 us (99%)
  between operations  0.64 us (1%)
    pallas_call x1, Pallas kernels, shards(): pl.pallas_call(kernel, out_shape=(jax.ShapeDtypeStruct((UB, SIDE, R), BF)...  55.2 us

profile of v4, /device:TPU:1, one launch (start us, length us, event | category | flops | bytes accessed | tf_op | source)
XLA Modules:
  0.0 56.9 jit_solution(6232302243534942690)
XLA Ops:
  0.6 55.2 %shard_map.77 = (bf16[8,128,512]{2,1,0:T(8,128)(2,1)S(1)}, f32[32,512]{1,0:T(8,128)S(1)}) custom-call(s32[3,2,8]{2,1,0:T(2,128)} %bitcast.11, s32[3]{0:T(128)} %bitcast.12, bf16[8,128,512]{2,1,0:T(8,128)(2,1)} %bitcast.8, f32[32,512]{1,0:T(8,128)} %items_in.1, bf16[24,128,128]{2,1,0:T(8,128)(2,1)} %bitcast.9, s32[24,16,128]{2,1,0:T(8,128)} %bitcast.10), custom_call_target="tpu_custom_call" | custom-call | tf_op jit(solution)/shard_map/pallas_call | solution.py:310
  55.9 1.0 %shard_map.78 = (bf16[8,128,512]{2,1,0:T(8,128)(2,1)}, f32[32,512]{1,0:T(8,128)}) custom-call(bf16[8,128,512]{2,1,0:T(8,128)(2,1)S(1)} %get-tuple-element.6.users_in, f32[32,512]{1,0:T(8,128)S(1)} %get-tuple-element.7.items_in), custom_call_target="tpu_custom_call" | custom-call | tf_op jit(solution)/shard_map/pallas_call | solution.py:362

commit v5 on v4

--- a/solution.py
+++ b/solution.py
@@ -19,21 +19,18 @@
 PIECE = 32
 UB, IB = 8, 4
 N_STRATA = 32
-H = 2
-PART = PIECE // H
-Q = J * H
 MARK = 1e30
 LIMIT = 1e20
 PEERS = [(2, 1), (1, 1), (3, 1), (2, 0), (0, 1), (1, 0), (3, 0)]
+NEXT = [(2, 1), (2, 0), (1, 1), (1, 0), (3, 1), (3, 0), (0, 1), (0, 0)]
 
 
 def kernel(
     blocks_in, counts_in, users_in, items_in, ratings_in, words_in,
     users_out, items_out,
     blocks, counts, users, items, ratings, words, marked, rates, panel0, panels, remaining, dense_t, grads,
-    u_own, u_out, u_in, y_out, y_in, x_out, x_in, r_out, r_in,
-    load_sem, pair_send, pair_recv, u_send, u_recv, n_send, n_recv, y_send, y_recv, x_send, x_recv,
-    r_send, r_recv, g_send, g_recv, i_send, i_recv,
+    u_own, u_out, u_in, a_out, r_out, r_in,
+    load_sem, pair_send, pair_recv, u_send, u_recv, n_send, n_recv, a_send, a_recv, r_send, r_recv, i_send, i_recv,
 ):
     s = lax.axis_index("strata")
     h = lax.axis_index("shard")
@@ -53,8 +50,8 @@
 
     barrier = pltpu.get_barrier_semaphore()
     partners = [mate] + [(s, at(dy, dx, c)) for dy, dx in PEERS]
-    partners += [(after, y * 4 + xx * 2 + c) for xx in range(NX)]
-    partners += [(before, y * 4 + xx * 2 + c) for xx in range(NX)]
+    partners += [(after, row(dy) * 4 + xx * 2 + c) for dy, xx in NEXT]
+    partners += [(before, row(dy) * 4 + xx * 2 + c) for dy, xx in NEXT]
     for partner in partners:
         pl.semaphore_signal(barrier, inc=1, device_id=partner, device_id_type=MESH)
 
@@ -88,28 +85,22 @@
         src, dst = pairs[n]
         return remote(src, dst.at[1], pair_send.at[n], pair_recv.at[n], mate)
 
-    def rows_of(q):
-        return pl.ds((q % H) * PART, PART)
-
-    def gather_y(t, q, dy, yy):
-        part = panels[t - 1][q // H].at[yy, :, rows_of(q)]
-        return remote(part, part, g_send.at[t - 1, q, dy - 1], g_recv.at[t - 1, q, dy - 1], (s, at(dy, 0, c)))
-
-    def reduce_y(t, q, dy):
+    def reduce(t, j, i):
+        dy, dx = PEERS[i]
+        return remote(r_out.at[t, j, i], r_in.at[t, j, i], r_send.at[t, j], r_recv.at[t, j], (s, at(dy, dx, c)))
+
+    def reduce_all(t, j):
+        return remote(r_out.at[t, j], r_in.at[t, j], r_send.at[t, j], r_recv.at[t, j], mate)
+
+    def advance(t, j, i):
+        dy, xx = NEXT[i]
         return remote(
-            y_out.at[t, q, dy - 1], y_in.at[t, q, dy - 1], y_send.at[t, q, dy - 1], y_recv.at[t, q, dy - 1],
-            (s, at(dy, 0, c)),
+            a_out.at[t, j], panels[t][j].at[y, x], a_send.at[t, j, i], a_recv.at[t, j],
+            (after, row(dy) * 4 + xx * 2 + c),
         )
 
-    def advance(t, q, xx, slot):
-        return remote(
-            x_out.at[t, q], x_in.at[t, q, slot], x_send.at[t, q, xx], x_recv.at[t, q, slot],
-            (after, y * 4 + xx * 2 + c),
-        )
-
-    def reduce_last(j, i):
-        dy, dx = PEERS[i]
-        return remote(r_out.at[j, i], r_in.at[j, i], r_send.at[j, i], r_recv.at[j, i], (s, at(dy, dx, c)))
+    def advance_all(t, j):
+        return remote(panels[t][j], panels[t][j], a_send.at[t, j, 0], a_recv.at[t, j], mate)
 
     def user_grads(t):
         return remote(u_out.at[t], u_in.at[t], u_send.at[t], u_recv.at[t], mate)
@@ -213,58 +204,38 @@
             grads[j] = jnp.dot(
                 dense_t[...], users[:, :, :, columns(j)].reshape(NC * UB * SIDE, W), preferred_element_type=F32
             ).reshape(NY, NX, PIECE, W)
+            for i, (dy, dx) in enumerate(PEERS):
+                r_out[t, j, i] = grads[j, row(dy), 1 - x if dx else x].astype(BF)
+                reduce(t, j, i).start()
+        send_user_grads(t)
+        if t == T - 1:
+            update_users(t)
+            out = pltpu.make_async_copy(users.at[0], users_out, load_sem.at[0])
+            out.start()
+        for j in range(J):
+            reduce_all(t, j).wait_recv()
+            total = grads[j, y, x]
+            for i in range(len(PEERS)):
+                total += r_in[t, j, i].astype(F32)
+            mine = panel_at(t, j, y, x).astype(F32) if t else items[:, columns(j)]
+            fresh = mine + step_item * (total - shrinkage * mine)
             if t < T - 1:
-                for q in range(j * H, (j + 1) * H):
-                    for dy in (2, 1, 3):
-                        y_out[t, q, dy - 1] = grads[j, row(dy), :, (q % H) * PART:(q % H + 1) * PART].astype(BF)
-                        reduce_y(t, q, dy).start()
+                a_out[t, j] = fresh.astype(BF)
+                for i in range(len(NEXT)):
+                    advance(t, j, i).start()
             else:
-                for i, (dy, dx) in enumerate(PEERS):
-                    r_out[j, i] = grads[j, row(dy), 1 - x if dx else x].astype(BF)
-                    reduce_last(j, i).start()
-        send_user_grads(t)
+                items[:, columns(j)] = fresh
         if t < T - 1:
-            for q in range(Q):
-                total = grads[q // H, y, :, (q % H) * PART:(q % H + 1) * PART]
-                for dy in (1, 3, 2):
-                    reduce_y(t, q, dy).wait_recv()
-                    total += y_in[t, q, dy - 1].astype(F32)
-                mine = panel_at(t, q // H, y, slice(None), slice((q % H) * PART, (q % H + 1) * PART)).astype(F32)
-                half = step_item * total + (0.5 * (1.0 - step_item * shrinkage)) * mine
-                x_out[t, q] = half.astype(BF)
-                for xx in range(NX):
-                    advance(t, q, xx, x).start()
             update_users(t)
             new_users(t).start()
-            for q in range(Q):
-                for xx in range(NX):
-                    advance(t, q, xx, xx).wait_recv()
-                both = x_in[t, q, 0].astype(F32) + x_in[t, q, 1].astype(F32)
-                panels[t][q // H][y, :, (q % H) * PART:(q % H + 1) * PART] = both.astype(BF)
-                for dy in (2, 1, 3):
-                    gather_y(t + 1, q, dy, y).start()
             for cc in range(NC):
                 mark(t + 1, cc)
             place(t + 1)
             new_users(t).wait_recv()
-            for q in range(H):
-                for dy in (1, 3, 2):
-                    gather_y(t + 1, q, dy, row(4 - dy)).wait_recv()
+            advance_all(t, 0).wait_recv()
             predict_first(t + 1)
-            for q in range(H, Q):
-                for dy in (1, 3, 2):
-                    gather_y(t + 1, q, dy, row(4 - dy)).wait_recv()
+            advance_all(t, 1).wait_recv()
         else:
-            update_users(t)
-            out = pltpu.make_async_copy(users.at[0], users_out, load_sem.at[0])
-            out.start()
-            for j in range(J):
-                total = grads[j, y, x]
-                for i in reversed(range(len(PEERS))):
-                    reduce_last(j, i).wait_recv()
-                    total += r_in[j, i].astype(F32)
-                mine = panel_at(t, j, y, x).astype(F32)
-                items[:, columns(j)] = mine + step_item * (total - shrinkage * mine)
             last = pltpu.make_async_copy(items, items_out, load_sem.at[1])
             last.start()
 
@@ -272,17 +243,13 @@
         share(n).wait_send()
     for i in range(len(PEERS)):
         first_copy(i, y, x).wait_send()
-        for j in range(J):
-            reduce_last(j, i).wait_send()
     for t in range(T):
         user_grads(t).wait_send()
-    for t in range(T - 1):
-        for q in range(Q):
-            for dy in (1, 2, 3):
-                reduce_y(t, q, dy).wait_send()
-                gather_y(t + 1, q, dy, y).wait_send()
-            for xx in range(NX):
-                advance(t, q, xx, x).wait_send()
+        for j in range(J):
+            reduce_all(t, j).wait_send()
+            if t < T - 1:
+                for i in range(len(NEXT)):
+                    advance(t, j, i).wait_send()
     out.wait()
     last.wait()
 
@@ -332,20 +299,15 @@
             vmem((UB, SIDE, R), F32),
             vmem((T, UB, SIDE, R), BF),
             vmem((T, UB, SIDE, R), BF),
-            vmem((T - 1, Q, 3, NX, PART, W), BF),
-            vmem((T - 1, Q, 3, NX, PART, W), BF),
-            vmem((T - 1, Q, NX, PART, W), BF),
-            vmem((T - 1, Q, NX, NX, PART, W), BF),
-            vmem((J, n, PIECE, W), BF),
-            vmem((J, n, PIECE, W), BF),
+            vmem((T - 1, J, PIECE, W), BF),
+            vmem((T, J, n, PIECE, W), BF),
+            vmem((T, J, n, PIECE, W), BF),
             dma((6,)),
             dma((5,)), dma((5,)),
             dma((T,)), dma((T,)),
             dma((T - 1,)), dma((T - 1,)),
-            dma((T - 1, Q, 3)), dma((T - 1, Q, 3)),
-            dma((T - 1, Q, NX)), dma((T - 1, Q, NX)),
-            dma((J, n)), dma((J, n)),
-            dma((T - 1, Q, 3)), dma((T - 1, Q, 3)),
+            dma((T - 1, J, len(NEXT))), dma((T - 1, J)),
+            dma((T, J)), dma((T, J)),
             dma((n,)), dma((n,)),
         ],
         compiler_params=pltpu.CompilerParams(

time: 57 us -> 57.4 us (level)
  no operation moved by 1% of the time
where the time goes in v5:
time: 57.4 us; the launch traced here: 57.3 us
  Pallas kernels  56.5 us (98%)
  between operations  0.8 us (1%)
    pallas_call x1, Pallas kernels, shards(): pl.pallas_call(kernel, out_shape=(jax.ShapeDtypeStruct((UB, SIDE, R), BF)...  55.5 us

profile of v5, /device:TPU:1, one launch (start us, length us, event | category | flops | bytes accessed | tf_op | source)
XLA Modules:
  0.0 57.3 jit_solution(7806973267810903239)
XLA Ops:
  0.6 55.5 %shard_map.77 = (bf16[8,128,512]{2,1,0:T(8,128)(2,1)S(1)}, f32[32,512]{1,0:T(8,128)S(1)}) custom-call(s32[3,2,8]{2,1,0:T(2,128)} %bitcast.11, s32[3]{0:T(128)} %bitcast.12, bf16[8,128,512]{2,1,0:T(8,128)(2,1)} %bitcast.8, f32[32,512]{1,0:T(8,128)} %items_in.1, bf16[24,128,128]{2,1,0:T(8,128)(2,1)} %bitcast.9, s32[24,16,128]{2,1,0:T(8,128)} %bitcast.10), custom_call_target="tpu_custom_call" | custom-call | tf_op jit(solution)/shard_map/pallas_call | solution.py:277
  56.1 1.0 %shard_map.78 = (bf16[8,128,512]{2,1,0:T(8,128)(2,1)}, f32[32,512]{1,0:T(8,128)}) custom-call(bf16[8,128,512]{2,1,0:T(8,128)(2,1)S(1)} %get-tuple-element.6.users_in, f32[32,512]{1,0:T(8,128)S(1)} %get-tuple-element.7.items_in), custom_call_target="tpu_custom_call" | custom-call | tf_op jit(solution)/shard_map/pallas_call | solution.py:324

commit v6 on v5

--- a/solution.py
+++ b/solution.py
@@ -41,7 +41,7 @@
     before = lax.rem(s + N_STRATA - 1, N_STRATA)
 
     def row(dy):
-        return lax.rem(y + dy, NY)
+        return lax.rem(y + dy + c * (NY - 2 * dy), NY)
 
     def at(dy, dx, cc):
         return row(dy) * 4 + (1 - x if dx else x) * 2 + cc
@@ -190,10 +190,11 @@
     for load in loads:
         load.wait()
     mark(0, 0)
-    for n in range(len(pairs)):
+    for n in range(len(pairs) - 1):
         share(n).wait_recv()
     mark(0, 1)
     place(0)
+    share(len(pairs) - 1).wait_recv()
     for i, (dy, dx) in enumerate(PEERS):
         first_copy(i, row(4 - dy), (1 - x if dx else x)).wait_recv()
     predict_first(0)
@@ -255,10 +256,10 @@
 
 
 def store(users_in, items_in, users_out, items_out, sem):
-    copies = [
-        pltpu.make_async_copy(users_in, users_out, sem.at[0]),
-        pltpu.make_async_copy(items_in, items_out, sem.at[1]),
-    ]
+    copies = [pltpu.make_async_copy(items_in, items_out, sem.at[0])]
+    for n in range(4):
+        part = pl.ds(n * UB // 4, UB // 4)
+        copies.append(pltpu.make_async_copy(users_in.at[part], users_out.at[part], sem.at[n + 1]))
     for copy in copies:
         copy.start()
     for copy in copies:
@@ -329,7 +330,7 @@
         ),
         in_specs=[space] * 2,
         out_specs=(pl.BlockSpec(memory_space=pltpu.HBM),) * 2,
-        scratch_shapes=[dma((2,))],
+        scratch_shapes=[dma((5,))],
         compiler_params=pltpu.CompilerParams(vmem_limit_bytes=1024 * 1024),
     )(users, panel)
     return users.reshape(UB * SIDE, R), panel

time: 57.4 us -> 55.5 us (0.967)
  Pallas kernels: 56.5 us -> 54.5 us
    pallas_call x1, Pallas kernels: 55.5 us -> 53.5 us  [shards(): pl.pallas_call(kernel, out_shape=(jax.ShapeDtypeStruct((UB, SIDE, R), BF)...]
where the time goes in v6:
time: 55.5 us; the launch traced here: 55.3 us
  Pallas kernels  54.5 us (98%)
  between operations  0.8 us (1%)
    pallas_call x1, Pallas kernels, shards(): pl.pallas_call(kernel, out_shape=(jax.ShapeDtypeStruct((UB, SIDE, R), BF)...  53.5 us

profile of v6, /device:TPU:1, one launch (start us, length us, event | category | flops | bytes accessed | tf_op | source)
XLA Modules:
  0.0 55.3 jit_solution(1395204998234664987)
XLA Ops:
  0.6 53.5 %shard_map.77 = (bf16[8,128,512]{2,1,0:T(8,128)(2,1)S(1)}, f32[32,512]{1,0:T(8,128)S(1)}) custom-call(s32[3,2,8]{2,1,0:T(2,128)} %bitcast.11, s32[3]{0:T(128)} %bitcast.12, bf16[8,128,512]{2,1,0:T(8,128)(2,1)} %bitcast.8, f32[32,512]{1,0:T(8,128)} %items_in.1, bf16[24,128,128]{2,1,0:T(8,128)(2,1)} %bitcast.9, s32[24,16,128]{2,1,0:T(8,128)} %bitcast.10), custom_call_target="tpu_custom_call" | custom-call | tf_op jit(solution)/shard_map/pallas_call | solution.py:278
  54.1 1.0 %shard_map.78 = (bf16[8,128,512]{2,1,0:T(8,128)(2,1)}, f32[32,512]{1,0:T(8,128)}) custom-call(bf16[8,128,512]{2,1,0:T(8,128)(2,1)S(1)} %get-tuple-element.6.users_in, f32[32,512]{1,0:T(8,128)S(1)} %get-tuple-element.7.items_in), custom_call_target="tpu_custom_call" | custom-call | tf_op jit(solution)/shard_map/pallas_call | solution.py:325
